TPU v7x, 128 devices: a whole 4x4x4 slice. The times are simulated.
128 devices in a mesh: replica: 16 (over y_lo, z, core), tensor: 8 (over y_hi, x).
Axes of the slice: x: 4, y: 4 (y_hi: 2, y_lo: 2; y = y_hi * 2 + y_lo), z: 4, core: 2. Of those that a mesh axis runs over, the one named last changes fastest.
Arguments:
- hidden: bfloat16 [128, 2, 8192], P('replica'), may hold values from -6 to 6
- shard_rows: float32 [8704, 18432], P(('replica', 'tensor')), may hold values from -0.0625 to 0.0625
- piece_length: int32 [128], replicated, may hold values from 1 to 68, 8192 in all
- cache_keys: bfloat16 [128, 8, 4096, 128], P('replica', 'tensor'), may hold values from -200 to 200
- cache_values: bfloat16 [128, 8, 4096, 128], P('replica', 'tensor'), may hold values from -6 to 6
- cache_fill: int32 [128], P('replica'), may hold values from 1 to 4096, as said below
Outputs:
- layer_out: bfloat16 [128, 2, 8192], P('replica', None, 'tensor')
Inputs may be any that keep to these rules, and one draw needn't show every extreme that they name: `piece_length`: the device with replica index r and tensor index t holds piece r times the tensor axis size plus t; some piece has exactly 68 rows. `cache_fill`: some row has a full cache.
All inputs are finite; a program needn't handle non-finite values.
Results may differ from a plain program's by a relative error of at most 0.014.
Values may be sent and summed in bfloat16 or wider, within the bound.
No kernel may reach another device: no remote copies, remote signals or barrier semaphores. Data moves between devices by JAX's collectives and lax.ppermute only.
A program may use at most 192 MiB of HBM per device.

v0:
```python
import math
import jax
import jax.numpy as jnp
from jax import lax
from jax.sharding import PartitionSpec as P

D = 8192
HQ = 64
KV = 8
HD = 128
ROPE_BASE = 1000000.0
NEG_FILL = -1e30


def rotate(source, position):
    halfway = source.shape[-1] // 2
    exponent = jnp.arange(halfway, dtype=jnp.float32) * (2.0 / source.shape[-1])
    frequency = jnp.exp(-exponent * math.log(ROPE_BASE))
    angles = position[:, None, None] * frequency[None, None, :]
    cosine = jnp.cos(angles)
    sine_part = jnp.sin(angles)
    former = source[..., :halfway]
    latter = source[..., halfway:]
    return jnp.concatenate(
        [former * cosine - latter * sine_part, latter * cosine + former * sine_part], axis=-1
    )


def attend(projected, keys_cache, values_cache, filled):
    batch_rows, heads_kv, span_len, head_size = keys_cache.shape
    count = projected.shape[0]
    width_kv = heads_kv * head_size
    width_q = projected.shape[1] - 2 * width_kv
    heads_q = width_q // head_size
    group_size = heads_q // heads_kv
    position = (
        (filled[:, None] + jnp.arange(2, dtype=jnp.int32)[None, :]).reshape(-1).astype(jnp.float32)
    )
    query = rotate(projected[:, :width_q].reshape(count, heads_q, head_size), position).astype(
        jnp.bfloat16
    )
    new_key = rotate(
        projected[:, width_q : width_q + width_kv].reshape(count, heads_kv, head_size), position
    ).astype(jnp.bfloat16)
    new_value = (
        projected[:, width_q + width_kv :]
        .astype(jnp.bfloat16)
        .reshape(batch_rows, 2, heads_kv, head_size)
    )
    query = query.reshape(batch_rows, 2, heads_kv, group_size, head_size)
    new_key = new_key.reshape(batch_rows, 2, heads_kv, head_size)
    factor = 1.0 / math.sqrt(head_size)
    cached = (
        jnp.einsum("bskgd,bkcd->bkgsc", query, keys_cache, preferred_element_type=jnp.float32)
        * factor
    )
    recent = (
        jnp.einsum("bskgd,btkd->bkgst", query, new_key, preferred_element_type=jnp.float32) * factor
    )
    visible = (jnp.arange(span_len)[None, :] < filled[:, None])[:, None, None, None, :]
    causal = jnp.arange(2)[:, None] >= jnp.arange(2)[None, :]
    cached = jnp.where(visible, cached, NEG_FILL)
    recent = jnp.where(causal, recent, NEG_FILL)
    highest = jnp.maximum(jnp.max(cached, axis=-1), jnp.max(recent, axis=-1))
    cached_exp = jnp.exp(cached - highest[..., None])
    recent_exp = jnp.exp(recent - highest[..., None])
    total = jnp.sum(cached_exp, axis=-1) + jnp.sum(recent_exp, axis=-1)
    cached_prob = (cached_exp / total[..., None]).astype(jnp.bfloat16)
    recent_prob = (recent_exp / total[..., None]).astype(jnp.bfloat16)
    mixed = jnp.einsum(
        "bkgsc,bkcd->bskgd", cached_prob, values_cache, preferred_element_type=jnp.float32
    )
    mixed = mixed + jnp.einsum(
        "bkgst,btkd->bskgd", recent_prob, new_value, preferred_element_type=jnp.float32
    )
    return mixed.astype(jnp.bfloat16).reshape(count, width_q)


def split_slices(block, slices, width_q, width_kv):
    height = block.shape[0]
    bounds = (0, width_q, width_q + width_kv, width_q + 2 * width_kv, block.shape[1])
    pieces = [
        block[:, bounds[index] : bounds[index + 1]].reshape(height, slices, -1)
        for index in range(4)
    ]
    return jnp.concatenate(pieces, axis=2).astype(jnp.bfloat16)


def padded_columns(matrix, piece_length, starts, capacity):
    offsets = jnp.arange(capacity, dtype=jnp.int32)
    source = (starts[:, None] + offsets[None, :]).reshape(-1)
    valid = (offsets[None, :] < piece_length[:, None]).reshape(-1)
    source = jnp.clip(source, 0, matrix.shape[1] - 1)
    picked = jnp.take(matrix, source, axis=1)
    return jnp.where(valid[None, :], picked, jnp.zeros((), matrix.dtype))


def model_order(padded, piece_ends, starts, capacity):
    global_row = jnp.arange(D, dtype=jnp.int32)
    passed = piece_ends[None, :] <= global_row[:, None]
    owners = jnp.sum(passed.astype(jnp.int32), axis=1)
    own_start = jnp.max(
        jnp.where(starts[None, :] <= global_row[:, None], starts[None, :], 0), axis=1
    )
    source = owners * capacity + (global_row - own_start)
    return jnp.take(padded, source, axis=1)


def body(hidden, shard_rows, piece_length, cache_keys, cache_values, cache_fill):
    slices = lax.axis_size("tensor")
    capacity = shard_rows.shape[0]
    batch_rows = cache_keys.shape[0]
    project_width = (HQ + 2 * KV) * HD // slices
    tokens = hidden.reshape(batch_rows * 2, hidden.shape[2])
    stacked = split_slices(shard_rows, slices, HQ * HD, KV * HD)
    received = lax.all_to_all(stacked, "tensor", split_axis=1, concat_axis=0, tiled=True).reshape(
        slices * capacity, -1
    )
    piece_ends = jnp.cumsum(piece_length)
    starts = piece_ends - piece_length
    gathered = lax.all_gather(received, "replica", axis=0, tiled=True)
    token_cols = padded_columns(tokens, piece_length, starts, capacity)
    projected = jnp.dot(token_cols, gathered[:, :project_width], preferred_element_type=jnp.float32)
    attended = attend(projected, cache_keys, cache_values, cache_fill)
    padded_out = jnp.einsum(
        "tf,jf->tj", attended, gathered[:, project_width:], preferred_element_type=jnp.float32
    )
    partial_value = model_order(padded_out, piece_ends, starts, capacity)
    result = lax.psum_scatter(
        partial_value.astype(jnp.bfloat16), "tensor", scatter_dimension=1, tiled=True
    )
    return result.reshape(batch_rows, 2, -1)


def solution(mesh):
    placed = (
        P("replica", None, None),
        P(("replica", "tensor"), None),
        P(),
        P("replica", "tensor", None, None),
        P("replica", "tensor", None, None),
        P("replica"),
    )
    return jax.shard_map(
        body, mesh=mesh, in_specs=placed, out_specs=P("replica", None, "tensor"), check_vma=False
    )
```

profile of v0, /device:TPU:0, one launch (start us, length us, event | category | flops | bytes accessed | tf_op | source)
XLA Modules:
  0.0 404.8 jit_solution(11453051769635122451)
XLA Ops:
  6.5 0.0 all-gather.2.cloned.1.call-start
  6.5 2.8 convert.33
  9.3 0.2 fusion.56
  9.5 0.7 copy.32
  10.2 0.1 slice.74
  10.3 0.6 copy.21
  10.9 0.7 copy.35
  11.6 0.1 slice.77
  11.7 0.6 copy.24
  12.5 0.2 pad_maximum_fusion
  12.7 41.8 %all_to_all.15 = bf16[68,8,2304]{2,0,1:T(8,128)(2,1)S(1)} all-to-all(bf16[68,8,2304]{2,0,1:T(8,128)(2,1)S(1)} %pad_maximum_fusion), channel_id=1, replica_groups=mesh['replica'=16,'tensor'=8] {'tensor'}, dimensions={1} | all-to-all | bytes 5013504 | tf_op jit(solution)/shard_map/all_to_all | solution.py:116
  54.5 2.2 reshape.409
  56.8 0.0 copy-start.1
  56.8 0.0 copy-start
  56.8 0.0 all-gather.2.cloned.1.call-update
  56.8 0.0 copy-start.2
  56.8 0.0 reduce-scatter.2.cloned.1.call-start
  56.9 0.6 copy-done.1
  57.4 0.1 copy.19
  57.5 0.2 reduce-window.8
  57.7 0.1 reduce.4
  57.8 0.1 add_clamp_fusion
  57.9 0.1 min.18
  58.1 0.1 min.16
  58.2 0.0 copy-done
  58.2 0.1 reshape.404
  58.3 1.0 copy.20
  59.3 0.1 iota_compare_fusion.3
  59.4 0.1 lt.85
  59.5 0.0 copy-done.2
  59.5 0.1 add_convert_fusion.1
  59.6 0.1 convert_element_type.44
  59.7 0.1 fusion.36
  59.8 18.3 %gather_fusion = bf16[8704,16]{1,0:T(8,128)(2,1)} fusion(bf16[16,8192]{0,1:T(8,128)(2,1)S(1)} %copy.20, s32[9216]{0:T(1024)S(1)} %pad_clamp_fusion), kind=kCustom, calls=%fused_computation | custom fusion | bytes 591872 | tf_op jit(solution)/shard_map/jit(_take)/gather | solution.py:94
  78.2 0.1 multiply_cosine_fusion.1
  78.3 2.2 select_reduce_fusion
  80.5 0.1 compare_select_fusion.1
  80.7 0.1 iota_compare_fusion.2
  80.8 175.7 %all-gather.2.cloned.1.call-done = bf16[8704,2304]{1,0:T(8,128)(2,1)} async-done(((bf16[544,2304]{1,0:T(8,128)(2,1)}), bf16[8704,2304]{1,0:T(8,128)(2,1)}) %all-gather.2.cloned.1.call-update) | async-done | bytes 40108048 | tf_op jit(solution)/shard_map/all_gather | solution.py:121
  256.5 10.1 %fusion = f32[16,1280]{1,0:T(8,128)S(1)} fusion(bf16[8704,2304]{1,0:T(8,128)(2,1)} %all-gather.2.cloned.1.call-done, bf16[8704,16]{1,0:T(8,128)(2,1)} %gather_fusion, pred[8704]{0:T(1024)(128)(4,1)S(1)} %lt.85, pred[8704]{0:T(1024)(128)(4,1)S(1)} %compare_and_fusion), kind=kOutput, calls=%fused_computation.2 | convolution fusion | flops 356794368 | bytes 24609792 | tf_op jit(solution)/shard_map/dot_general | solution.py:123
  266.6 0.1 fusion.45
  266.8 0.1 subtract_convert_fusion
  266.9 5.8 %fusion.58 = (f32[8,8,2]{1,2,0:T(2,128)S(1)}, f32[8,1,8,2,4096]{4,2,3,0,1:T(8,128)S(1)}) fusion(bf16[8,1,4096,128]{3,2,1,0:T(8,128)(2,1)} %param.9, bf16[8,2,8,64]{3,2,1,0:T(8,128)(2,1)S(1)} %bitcast.115, bf16[8,2,8,64]{3,2,1,0:T(8,128)(2,1)S(1)} %bitcast.113, pred[8,4096]{1,0:T(8,128)(4,1)S(1)} %iota_compare_fusion.2), kind=kOutput, calls=%fused_computation.88 | convolution fusion | flops 135856000 | bytes 10551808 | tf_op jit(solution)/shard_map/bskgd,bkcd->bkgsc/dot_general | solution.py:54
  272.7 0.4 fusion.59
  273.1 0.4 fusion.25
  273.5 4.7 %fusion.26 = f32[8,128,8,2]{1,2,3,0:T(8,128)S(1)} fusion(bf16[8,1,4096,128]{3,2,1,0:T(8,128)(2,1)} %param.10, f32[8,1,8,2,4096]{4,2,3,0,1:T(8,128)S(1)} %get-tuple-element.16, f32[8,8,2]{1,2,0:T(2,128)S(1)} %add.134, f32[8,8,2]{1,2,0:T(2,128)S(1)} %max.22), kind=kOutput, calls=%fused_computation.28 | convolution fusion | flops 135790592 | bytes 10552320 | tf_op jit(solution)/shard_map/bkgsc,bkcd->bskgd/dot_general | solution.py:70
  278.2 0.2 fusion.29
  278.5 12.5 %fusion.2 = bf16[16,8704]{0,1:T(8,128)(2,1)} fusion(bf16[8704,2304]{1,0:T(8,128)(2,1)} %all-gather.2.cloned.1.call-done, bf16[2,8,8,128]{3,2,1,0:T(8,128)(2,1)S(1)} %bitcast.123), kind=kOutput, calls=%fused_computation.4 | convolution fusion | flops 285212672 | bytes 18137088 | tf_op jit(solution)/shard_map/tf,jf->tj/dot_general | solution.py:125
  291.0 23.8 %gather_fusion.1 = bf16[8192,16]{1,0:T(8,128)(2,1)S(1)} fusion(bf16[16,8704]{0,1:T(8,128)(2,1)} %fusion.2, s32[8192]{0:T(1024)S(1)} %broadcast_clamp_fusion), kind=kCustom, calls=%fused_computation.1 | custom fusion | bytes 557056 | tf_op jit(solution)/shard_map/jit(_take)/gather | solution.py:106
  314.8 5.0 %fusion.24 = bf16[16,8192]{0,1:T(8,128)(2,1)} fusion(bf16[8192,16]{1,0:T(8,128)(2,1)S(1)} %gather_fusion.1, pred[8192]{0:T(1024)(128)(4,1)S(1)} %compare_and_fusion.1), kind=kLoop, calls=%fused_computation.24 | loop fusion | flops 131072 | bytes 532480 | tf_op jit(solution)/shard_map/convert_element_type | solution.py:130
  319.9 0.0 reduce-scatter.2.cloned.1.call-update
  319.9 76.4 %reduce-scatter.2.cloned.1.call-done = bf16[16,1024]{0,1:T(8,128)(2,1)} async-done(((bf16[16,8192]{0,1:T(8,128)(2,1)}), bf16[16,1024]{0,1:T(8,128)(2,1)}) %reduce-scatter.2.cloned.1.call-update) | async-done | bytes 32784 | tf_op jit(solution)/shard_map/reduce_scatter | solution.py:129
  396.3 1.0 copy.26
  397.3 0.6 reshape.418
  (22 shorter events, 0.3 us)
Async XLA Ops:
  6.5 250.0 %all-gather.2.cloned.1.call-start = ((), (), s32[]{:S(2)}) async-start(), calls=%async_computation.2 | async-start | bytes 42614784 | tf_op jit(solution)/shard_map/all_gather | solution.py:121
  56.8 0.7 copy-start.1
  56.8 1.4 copy-start
  56.8 2.7 copy-start.2
  56.8 339.5 %reduce-scatter.2.cloned.1.call-start = ((), (), s32[]{:S(2)}) async-start(), calls=%async_computation.3 | async-start | bytes 2359296 | tf_op jit(solution)/shard_map/reduce_scatter | solution.py:129
Sparse Core Ops, SparseCore 0:
  56.9 199.5 all-gather.1
  320.0 76.2 reduce-scatter.1
where the time goes:
time: 405 us
  waiting for transfers between devices  252 us (62%)
  local copies, waits for them, and re-layouts  51.4 us (13%)
  blocking collectives  41.8 us (10%)
  matrix products  33.7 us (8%)
  between operations  13.8 us (3%)
  other arithmetic  12 us (3%)
    all_gather x1, waiting for transfers between devices, body(): gathered = lax.all_gather(received, 'replica', axis=0, tiled=True)  176 us
    reduce_scatter x1, waiting for transfers between devices, body(): lax.psum_scatter(partial_value.astype(jnp.bfloat16), 'tensor', scatter_di...  76.4 us
    all_to_all x1, blocking collectives, body(): lax.all_to_all(stacked, 'tensor', split_axis=1, concat_axis=0, tiled=True)  41.8 us
    gather x1, local copies, waits for them, and re-layouts, model_order(): return jnp.take(padded, source, axis=1)  23.8 us
    gather x1, local copies, waits for them, and re-layouts, padded_columns(): picked = jnp.take(matrix, source, axis=1)  18.3 us
    dot_general x1, matrix products, body(): jnp.einsum('tf,jf->tj', attended, gathered[:, project_width:], preferred_...  12.5 us
    dot_general x1, matrix products, body(): jnp.dot(token_cols, gathered[:, :project_width], preferred_element_type=j...  10.1 us
  transfers between devices with their start and end apart: 2, of which 2 were waited for; matrix products, arithmetic and copies ran while one was open for 6% of the time, Pallas kernels for 0%

commit v1 on v0

--- a/solution.py
+++ b/solution.py
@@ -118,7 +118,9 @@
     )
     piece_ends = jnp.cumsum(piece_length)
     starts = piece_ends - piece_length
-    gathered = lax.all_gather(received, "replica", axis=0, tiled=True)
+    gathered = jnp.concatenate(
+        lax.all_to_all(jnp.stack([received] * lax.axis_size("replica")), "replica", 0, 0), axis=0
+    )
     token_cols = padded_columns(tokens, piece_length, starts, capacity)
     projected = jnp.dot(token_cols, gathered[:, :project_width], preferred_element_type=jnp.float32)
     attended = attend(projected, cache_keys, cache_values, cache_fill)

time: 405 us -> 850 us (2.10)
  waiting for transfers between devices: 252 us -> 678 us
  local copies, waits for them, and re-layouts: 51.4 us -> 64.9 us
    all_to_all x0 -> x1, waiting for transfers between devices: none -> 605 us  [body(): lax.all_to_all(jnp.stack([received] * lax.axis_size('replica')), 'replica...]
    all_gather x1 -> x0, waiting for transfers between devices: 176 us -> none  [body(): gathered = lax.all_gather(received, 'replica', axis=0, tiled=True)]
    another operation x1 -> x3, local copies, waits for them, and re-layouts: 0.11 us -> 16.5 us  [the longest x2 16.4 us: body(): jnp.stack([received] * lax.axis_size('replica'))]
  transfers between devices with their start and end apart: 2 -> 2, of which waited for: 2 -> 2; matrix products, arithmetic and copies ran while one was open for 6% -> 3% of each run, Pallas kernels for 0% -> 0%
where the time goes in v1:
time: 850 us; the launch traced here: 849 us
  waiting for transfers between devices  678 us (80%)
  local copies, waits for them, and re-layouts  64.9 us (8%)
  blocking collectives  41.8 us (5%)
  matrix products  31.9 us (4%)
  between operations  13.8 us (2%)
  other arithmetic  12 us (1%)
    all_to_all x1, waiting for transfers between devices, body(): lax.all_to_all(jnp.stack([received] * lax.axis_size('replica')), 'replica...  605 us
    reduce_scatter x1, waiting for transfers between devices, body(): lax.psum_scatter(partial_value.astype(jnp.bfloat16), 'tensor', scatter_di...  73.8 us
    all_to_all x1, blocking collectives, body(): lax.all_to_all(stacked, 'tensor', split_axis=1, concat_axis=0, tiled=True)  41.8 us
    gather x1, local copies, waits for them, and re-layouts, model_order(): return jnp.take(padded, source, axis=1)  23.8 us
    gather x1, local copies, waits for them, and re-layouts, padded_columns(): picked = jnp.take(matrix, source, axis=1)  18.3 us
  transfers between devices with their start and end apart: 2, of which 2 were waited for; matrix products, arithmetic and copies ran while one was open for 3% of the time, Pallas kernels for 0%

profile of v1, /device:TPU:0, one launch (start us, length us, event | category | flops | bytes accessed | tf_op | source)
XLA Modules:
  0.0 849.2 jit_solution(17218480037993770442)
XLA Ops:
  6.5 2.8 convert.33
  9.3 0.2 fusion.56
  9.5 0.7 copy.32
  10.2 0.1 slice.74
  10.3 0.6 copy.21
  10.9 0.7 copy.35
  11.6 0.1 slice.77
  11.7 0.6 copy.24
  12.5 0.2 pad_maximum_fusion
  12.7 41.8 %all_to_all.20 = bf16[68,8,2304]{2,0,1:T(8,128)(2,1)S(1)} all-to-all(bf16[68,8,2304]{2,0,1:T(8,128)(2,1)S(1)} %pad_maximum_fusion), channel_id=1, replica_groups=mesh['replica'=16,'tensor'=8] {'tensor'}, dimensions={1} | all-to-all | bytes 5013504 | tf_op jit(solution)/shard_map/all_to_all | solution.py:116
  54.5 2.1 stack_reshape.2
  56.7 14.3 %stack.3 = bf16[16,544,2304]{2,1,0:T(8,128)(2,1)} broadcast(bf16[544,2304]{1,0:T(8,128)(2,1)} %stack_reshape.2), dimensions={1,2} | broadcast | bytes 42614784 | tf_op jit(solution)/shard_map/stack | solution.py:122
  70.9 0.0 copy-start.1
  70.9 0.0 copy-start
  70.9 6.3 all-to-all-start.1
  77.3 0.0 copy-start.2
  77.3 0.0 reduce-scatter.2.cloned.1.call-start
  77.3 0.0 copy-done.1
  77.4 0.1 copy.19
  77.5 0.2 reduce-window.8
  77.6 0.1 reduce.4
  77.8 0.1 add_clamp_fusion
  77.9 0.1 min.18
  78.0 0.1 min.16
  78.1 0.0 copy-done
  78.1 0.1 reshape.406
  78.2 1.0 copy.20
  79.3 0.1 iota_compare_fusion.3
  79.3 0.1 lt.85
  79.5 0.0 copy-done.2
  79.5 0.1 add_convert_fusion.1
  79.5 0.1 convert_element_type.44
  79.6 0.1 fusion.36
  79.8 18.3 %gather_fusion = bf16[8704,16]{1,0:T(8,128)(2,1)} fusion(bf16[16,8192]{0,1:T(8,128)(2,1)S(1)} %copy.20, s32[9216]{0:T(1024)S(1)} %pad_clamp_fusion), kind=kCustom, calls=%fused_computation | custom fusion | bytes 591872 | tf_op jit(solution)/shard_map/jit(_take)/gather | solution.py:94
  98.0 0.1 multiply_cosine_fusion.1
  98.2 2.2 select_reduce_fusion
  100.4 0.1 compare_select_fusion.1
  100.5 0.1 iota_compare_fusion.2
  100.6 604.6 %all-to-all-done.1 = bf16[16,544,2304]{2,1,0:T(8,128)(2,1)} async-done(((bf16[16,544,2304]{2,1,0:T(8,128)(2,1)}), bf16[16,544,2304]{2,1,0:T(8,128)(2,1)}, u32[]{:S(2)}, u32[]{:S(2)}) %all-to-all-start.1) | async-done | bytes 40108064 | tf_op jit(solution)/shard_map/all_to_all | solution.py:122
  705.2 0.0 slice-start
  705.2 0.0 slice-start.1
  705.2 11.7 %fusion = f32[16,1280]{1,0:T(8,128)S(1)} fusion(bf16[8704,2304]{1,0:T(8,128)(2,1)} %bitcast.3, bf16[8704,16]{1,0:T(8,128)(2,1)} %gather_fusion, pred[8704]{0:T(1024)(128)(4,1)S(1)} %lt.85, pred[8704]{0:T(1024)(128)(4,1)S(1)} %compare_and_fusion), kind=kOutput, calls=%fused_computation.2 | convolution fusion | flops 356794368 | bytes 24609792 | tf_op jit(solution)/shard_map/dot_general | solution.py:125
  717.0 0.1 fusion.45
  717.1 0.1 subtract_convert_fusion
  717.2 0.0 slice-done
  717.2 0.0 slice-done.1
  717.2 2.4 fusion.58
  719.7 0.4 fusion.59
  720.1 0.4 fusion.25
  720.5 4.7 fusion.26
  725.2 0.2 fusion.29
  725.4 12.5 %fusion.2 = bf16[16,8704]{0,1:T(8,128)(2,1)} fusion(bf16[8704,2304]{1,0:T(8,128)(2,1)} %bitcast.3, bf16[2,8,8,128]{3,2,1,0:T(8,128)(2,1)S(1)} %bitcast.126), kind=kOutput, calls=%fused_computation.4 | convolution fusion | flops 285212672 | bytes 18137088 | tf_op jit(solution)/shard_map/tf,jf->tj/dot_general | solution.py:127
  738.0 23.8 %gather_fusion.1 = bf16[8192,16]{1,0:T(8,128)(2,1)S(1)} fusion(bf16[16,8704]{0,1:T(8,128)(2,1)} %fusion.2, s32[8192]{0:T(1024)S(1)} %broadcast_clamp_fusion), kind=kCustom, calls=%fused_computation.1 | custom fusion | bytes 557056 | tf_op jit(solution)/shard_map/jit(_take)/gather | solution.py:106
  761.8 5.0 fusion.24
  766.8 0.0 reduce-scatter.2.cloned.1.call-update
  766.9 73.8 %reduce-scatter.2.cloned.1.call-done = bf16[16,1024]{0,1:T(8,128)(2,1)} async-done(((bf16[16,8192]{0,1:T(8,128)(2,1)}), bf16[16,1024]{0,1:T(8,128)(2,1)}) %reduce-scatter.2.cloned.1.call-update) | async-done | bytes 32784 | tf_op jit(solution)/shard_map/reduce_scatter | solution.py:131
  840.6 1.0 copy.26
  841.7 0.6 reshape.420
  (23 shorter events, 0.3 us)
Async XLA Ops:
  70.9 6.4 copy-start.1
  70.9 7.2 copy-start
  70.9 634.3 %all-to-all-start.1 = ((bf16[16,544,2304]{2,1,0:T(8,128)(2,1)}), bf16[16,544,2304]{2,1,0:T(8,128)(2,1)}, u32[]{:S(2)}, u32[]{:S(2)}) async-start(bf16[16,544,2304]{2,1,0:T(8,128)(2,1)} %stack.3), calls=%async_computation.1 | async-start | bytes 80216064 | tf_op jit(solution)/shard_map/all_to_all | solution.py:122
  77.3 2.2 copy-start.2
  77.3 763.3 %reduce-scatter.2.cloned.1.call-start = ((), (), s32[]{:S(2)}) async-start(), calls=%async_computation.3 | async-start | bytes 2359296 | tf_op jit(solution)/shard_map/reduce_scatter | solution.py:131
  705.2 12.0 %slice-start = ((s8[8388608]{0:T(1024)(128)(4,1)}), s8[4194304]{0:T(1024)(128)(4,1)S(1)}, s32[]{:S(2)}) async-start(s8[8388608]{0:T(1024)(128)(4,1)} %bitcast.104), calls=%async_computation.4 | async-start | bytes 8388608
  705.2 12.0 %slice-start.1 = ((s8[8388608]{0:T(1024)(128)(4,1)}), s8[4194304]{0:T(1024)(128)(4,1)S(1)}, s32[]{:S(2)}) async-start(s8[8388608]{0:T(1024)(128)(4,1)} %bitcast.104), calls=%async_computation.5 | async-start | bytes 8388608
Sparse Core Ops, SparseCore 0:
  767.0 73.6 reduce-scatter.1
